TPU v7x, 32 devices: a whole 2x2x4 slice. The times are simulated.
32 devices in a mesh: section: 2 (over x), dp: 16 (over z, y, core).
Axes of the slice: x: 2, y: 2, z: 4, core: 2. Of those that a mesh axis runs over, the one named last changes fastest.
Arguments:
- edge_data: bfloat16 [2, 2, 1024, 960], P('section', None, 'dp'), may hold values from -6 to 6
- segment_ids: int32 [2, 1024], P(None, 'dp'), may hold values from 0 to 63, as said below
- attn_weight: bfloat16 [2, 960, 2560], P('section', None, 'dp'), may hold values from -0.1875 to 0.1875
- ffn_weight: bfloat16 [2, 3, 960, 2560], P('section', None, None, 'dp'), may hold values from -0.1875 to 0.1875
- gains: bfloat16 [2, 1920], P('section', 'dp'), may hold values from 0.5 to 1.5
Outputs:
- edge_out: bfloat16 [2, 2, 1024, 960], P('section', None, 'dp')
- attention_grad: float32 [2, 960, 2560], P('section', None, 'dp')
- ffn_grad: float32 [2, 3, 960, 2560], P('section', None, None, 'dp')
- gain_grad: float32 [2, 1920], P('section', 'dp')
Inputs may be any that keep to these rules, and one draw needn't show every extreme that they name: `segment_ids`: inside each aligned block of 64 tokens (one index of dp in one micro-batch) the ids start at 0 at the block's first token and rise by 0 or 1 from token to token; tokens of a block with equal ids form one sequence; no sequence crosses a block; some sequence fills a whole block, and some block holds only sequences of one token.
All inputs are finite; a program needn't handle non-finite values.
Results may differ from a plain program's by a relative error of at most 0.02.
Values may be sent and summed in bfloat16 or wider, within the bound.
No kernel may reach another device: no remote copies, remote signals or barrier semaphores. Data moves between devices by JAX's collectives and lax.ppermute only.
A program may use at most 256 MiB of HBM per device.

v0:
```python
import jax
import jax.numpy as jnp
from jax import lax
from jax.sharding import PartitionSpec as P

QUERY_HEADS = 15
KEY_VALUE_HEADS = 5
HEAD_SIZE = 64
epsilon = 1e-05
theta_base = 100000.0
contract_last = (((1,), (1,)), ((), ()))
contract_first = (((0,), (0,)), ((), ()))


def passed_along(array, axis, by):
    length = lax.axis_size(axis)
    pairs = [(i, i + by) for i in range(length) if 0 <= i + by < length]
    return lax.ppermute(array, axis, pairs)


def matmul(left_op, right_op):
    return jnp.dot(left_op, right_op, preferred_element_type=jnp.float32)


def right_trans(left_op, right_op):
    return lax.dot_general(left_op, right_op, contract_last, preferred_element_type=jnp.float32)


def left_trans(left_op, right_op):
    return lax.dot_general(left_op, right_op, contract_first, preferred_element_type=jnp.float32)


def norm_rows(rows, gain):
    return rows * lax.rsqrt(jnp.mean(rows * rows, axis=-1, keepdims=True) + epsilon) * gain


def rotary_apply(rows, cosine_table, sine_values):
    half_size = rows.shape[-1] // 2
    front_part = rows[..., :half_size]
    back_part = rows[..., half_size:]
    return jnp.concatenate(
        [
            front_part * cosine_table - back_part * sine_values,
            back_part * cosine_table + front_part * sine_values,
        ],
        axis=-1,
    )


def block_tables(segments):
    block_len = segments.shape[-1]
    offsets = jnp.arange(block_len, dtype=jnp.int32)
    same_segment = segments[..., :, None] == segments[..., None, :]
    segment_start = jnp.min(jnp.where(same_segment, offsets, block_len), axis=-1)
    positions = (offsets - segment_start).astype(jnp.float32)
    half_size = HEAD_SIZE // 2
    frequency = theta_base ** (-(2.0 * jnp.arange(half_size, dtype=jnp.float32)) / HEAD_SIZE)
    angles = positions[..., None] * frequency
    allowed = same_segment & (offsets[:, None] >= offsets[None, :])
    return (jnp.cos(angles), jnp.sin(angles), allowed)


def attention_scores(query_matrix, key_matrix_rows, allowed):
    scores = jnp.einsum(
        "tgrd,ugd->grtu", query_matrix, key_matrix_rows, preferred_element_type=jnp.float32
    ) * HEAD_SIZE ** (-0.5)
    return jnp.where(allowed, scores, -1000000000.0)


def layer_forward(layer_in, qkv_w, out_w, ffn_w, gain_row, cosine_table, sine_values, allowed):
    sequence_length, model_width = layer_in.shape
    head_column_width = QUERY_HEADS * HEAD_SIZE
    key_value_width = KEY_VALUE_HEADS * HEAD_SIZE
    query_group_count = QUERY_HEADS // KEY_VALUE_HEADS
    residual = layer_in.astype(jnp.float32)
    normed = norm_rows(residual, gain_row[:model_width].astype(jnp.float32)).astype(jnp.bfloat16)
    projected_rows = matmul(normed, qkv_w)
    query_matrix = rotary_apply(
        projected_rows[:, :head_column_width].reshape(
            sequence_length, KEY_VALUE_HEADS, query_group_count, HEAD_SIZE
        ),
        cosine_table[:, None, None, :],
        sine_values[:, None, None, :],
    ).astype(jnp.bfloat16)
    key_matrix_rows = rotary_apply(
        projected_rows[:, head_column_width : head_column_width + key_value_width].reshape(
            sequence_length, KEY_VALUE_HEADS, HEAD_SIZE
        ),
        cosine_table[:, None, :],
        sine_values[:, None, :],
    ).astype(jnp.bfloat16)
    value_matrix_rows = (
        projected_rows[:, head_column_width + key_value_width :]
        .reshape(sequence_length, KEY_VALUE_HEADS, HEAD_SIZE)
        .astype(jnp.bfloat16)
    )
    masked = attention_scores(query_matrix, key_matrix_rows, allowed)
    peak_score = jnp.max(masked, axis=-1, keepdims=True)
    log_total = peak_score + jnp.log(jnp.sum(jnp.exp(masked - peak_score), axis=-1, keepdims=True))
    prob_low = jnp.exp(masked - log_total).astype(jnp.bfloat16)
    attended = jnp.einsum(
        "grtu,ugd->tgrd", prob_low, value_matrix_rows, preferred_element_type=jnp.float32
    )
    attended = attended.reshape(sequence_length, head_column_width).astype(jnp.bfloat16)
    hidden = residual + right_trans(attended, out_w)
    normed_two = norm_rows(hidden, gain_row[model_width:].astype(jnp.float32)).astype(jnp.bfloat16)
    gate_proj = matmul(normed_two, ffn_w[0])
    upward = matmul(normed_two, ffn_w[1])
    active = (jax.nn.silu(gate_proj) * upward).astype(jnp.bfloat16)
    output = hidden + right_trans(active, ffn_w[2])
    saved_state = (
        residual,
        normed,
        query_matrix,
        key_matrix_rows,
        value_matrix_rows,
        log_total,
        attended,
        hidden,
        normed_two,
        gate_proj,
        upward,
        active,
    )
    return (output, saved_state)


def layer_backward(
    grad_out, saved_state, qkv_w, out_w, ffn_w, gain_row, cosine_table, sine_values, allowed
):
    (
        residual,
        normed,
        query_matrix,
        key_matrix_rows,
        value_matrix_rows,
        log_total,
        attended,
        hidden,
        normed_two,
        gate_proj,
        upward,
        active,
    ) = saved_state
    sequence_length, model_width = residual.shape
    head_column_width = QUERY_HEADS * HEAD_SIZE
    key_value_width = KEY_VALUE_HEADS * HEAD_SIZE
    query_group_count = QUERY_HEADS // KEY_VALUE_HEADS
    branch_grad = grad_out.astype(jnp.bfloat16)
    active_grad = matmul(branch_grad, ffn_w[2])
    _, pull_back = jax.vjp(lambda gate_in, up_in: jax.nn.silu(gate_in) * up_in, gate_proj, upward)
    gate_grad, up_grad = pull_back(active_grad)
    gate_grad = gate_grad.astype(jnp.bfloat16)
    up_grad = up_grad.astype(jnp.bfloat16)
    normed_two_grad = right_trans(gate_grad, ffn_w[0]) + right_trans(up_grad, ffn_w[1])
    _, pull_back = jax.vjp(norm_rows, hidden, gain_row[model_width:].astype(jnp.float32))
    hidden_part, gain_two_grad = pull_back(normed_two_grad)
    hidden_grad = grad_out + hidden_part
    mixed_grad = hidden_grad.astype(jnp.bfloat16)
    attended_grad = (
        matmul(mixed_grad, out_w)
        .reshape(sequence_length, KEY_VALUE_HEADS, query_group_count, HEAD_SIZE)
        .astype(jnp.bfloat16)
    )
    prob_full = jnp.exp(attention_scores(query_matrix, key_matrix_rows, allowed) - log_total)
    prob_low = prob_full.astype(jnp.bfloat16)
    value_grad = jnp.einsum(
        "grtu,tgrd->ugd", prob_low, attended_grad, preferred_element_type=jnp.float32
    )
    prob_grad = jnp.einsum(
        "tgrd,ugd->grtu", attended_grad, value_matrix_rows, preferred_element_type=jnp.float32
    )
    scores_grad = (
        prob_full * (prob_grad - jnp.sum(prob_grad * prob_full, axis=-1, keepdims=True))
    ).astype(jnp.bfloat16)
    query_grad = jnp.einsum(
        "grtu,ugd->tgrd", scores_grad, key_matrix_rows, preferred_element_type=jnp.float32
    ) * HEAD_SIZE ** (-0.5)
    key_grad = jnp.einsum(
        "grtu,tgrd->ugd", scores_grad, query_matrix, preferred_element_type=jnp.float32
    ) * HEAD_SIZE ** (-0.5)
    _, pull_back = jax.vjp(
        lambda rows: rotary_apply(
            rows, cosine_table[:, None, None, :], sine_values[:, None, None, :]
        ),
        query_grad,
    )
    (query_grad,) = pull_back(query_grad)
    _, pull_back = jax.vjp(
        lambda rows: rotary_apply(rows, cosine_table[:, None, :], sine_values[:, None, :]), key_grad
    )
    (key_grad,) = pull_back(key_grad)
    qkv_grad = jnp.concatenate(
        [
            query_grad.reshape(sequence_length, head_column_width),
            key_grad.reshape(sequence_length, key_value_width),
            value_grad.reshape(sequence_length, key_value_width),
        ],
        axis=1,
    ).astype(jnp.bfloat16)
    normed_grad = right_trans(qkv_grad, qkv_w)
    _, pull_back = jax.vjp(norm_rows, residual, gain_row[:model_width].astype(jnp.float32))
    input_part, gain_one_grad = pull_back(normed_grad)
    input_grad = hidden_grad + input_part
    pieces = (
        normed,
        qkv_grad,
        mixed_grad,
        attended,
        normed_two,
        gate_grad,
        up_grad,
        branch_grad,
        active,
    )
    return (input_grad, pieces, jnp.concatenate([gain_one_grad, gain_two_grad]))


def owner_rows_maker(piece_group, owners):
    joined = tuple(
        (jnp.concatenate([pieces[member] for pieces in piece_group], axis=0) for member in range(9))
    )
    normed, qkv_grad, mixed_grad, attended, normed_two, gate_grad, up_grad, branch_grad, active = (
        joined
    )
    token_count = normed.shape[0]
    qkv_cols = qkv_grad.shape[1]
    out_cols = attended.shape[1]
    qkv_padded = jnp.concatenate(
        [qkv_grad, jnp.zeros((token_count, out_cols), jnp.bfloat16)], axis=1
    )
    out_padded = jnp.concatenate(
        [jnp.zeros((token_count, qkv_cols), jnp.bfloat16), attended], axis=1
    )
    attn_share = (qkv_cols + out_cols) // owners
    ffn_share = gate_grad.shape[1] // owners
    owner_width = attn_share + 3 * ffn_share

    def one_owner(owner):
        attn_first = lax.dynamic_slice_in_dim(qkv_padded, owner * attn_share, attn_share, 1)
        attn_second = lax.dynamic_slice_in_dim(out_padded, owner * attn_share, attn_share, 1)
        attn_rows = left_trans(attn_first, normed) + left_trans(attn_second, mixed_grad)
        gate_rows = left_trans(
            lax.dynamic_slice_in_dim(gate_grad, owner * ffn_share, ffn_share, 1), normed_two
        )
        up_rows = left_trans(
            lax.dynamic_slice_in_dim(up_grad, owner * ffn_share, ffn_share, 1), normed_two
        )
        down_rows = left_trans(
            lax.dynamic_slice_in_dim(active, owner * ffn_share, ffn_share, 1), branch_grad
        )
        return jnp.concatenate([attn_rows, gate_rows, up_rows, down_rows], axis=0)

    def owner_rows(start, count):
        block_total = count // owner_width
        first_owner = start // owner_width
        owner_list = jnp.arange(block_total, dtype=jnp.int32)
        stacked = lax.map(one_owner, owner_list)
        return stacked.reshape(count, stacked.shape[-1])

    return (owner_rows, owner_width, attn_share, ffn_share)


def unpack_shard(shard, attn_share, ffn_share):
    attention_shard = shard[:attn_share].T[None]
    gate_part = shard[attn_share : attn_share + ffn_share].T
    up_part = shard[attn_share + ffn_share : attn_share + 2 * ffn_share].T
    down_part = shard[attn_share + 2 * ffn_share :].T
    return (attention_shard, jnp.stack([gate_part, up_part, down_part])[None])


def pick_section(leading, first_tree, second_tree):
    return jax.tree.map(
        lambda one_val, two_val: jnp.where(leading, one_val, two_val), first_tree, second_tree
    )


def local(edge_data, segment_ids, attn_weight, ffn_weight, gains):
    micro_count = segment_ids.shape[0]
    owners = lax.axis_size("dp")
    split_at = QUERY_HEADS * HEAD_SIZE + 2 * KEY_VALUE_HEADS * HEAD_SIZE
    leading = lax.axis_index("section") == 0
    table_list = [block_tables(segment_ids[mb_num]) for mb_num in range(micro_count)]
    gathered = (
        lax.all_gather(attn_weight, "dp", axis=2, tiled=True),
        lax.all_gather(ffn_weight, "dp", axis=3, tiled=True),
        lax.all_gather(gains, "dp", axis=1, tiled=True),
    )
    qkv_w = gathered[0][0][:, :split_at]
    out_w = gathered[0][0][:, split_at:]
    ffn_w, gain_row = (gathered[1][0], gathered[2][0])
    received = jnp.zeros_like(edge_data[0, 0])
    saved_list = []
    output_list = []
    for tick_num in range(micro_count + 1):
        own_input = edge_data[0, min(tick_num, micro_count - 1)]
        layer_in = jnp.where(leading, own_input, received)
        cosine_table, sine_values, allowed = pick_section(
            leading, table_list[min(tick_num, micro_count - 1)], table_list[max(tick_num - 1, 0)]
        )
        output, saved_state = layer_forward(
            layer_in, qkv_w, out_w, ffn_w, gain_row, cosine_table, sine_values, allowed
        )
        saved_list.append(saved_state)
        output_list.append(output)
        if tick_num < micro_count:
            received = passed_along(output.astype(jnp.bfloat16), "section", 1)
    back_weights = (
        lax.all_gather(attn_weight, "dp", axis=2, tiled=True),
        lax.all_gather(ffn_weight, "dp", axis=3, tiled=True),
        lax.all_gather(gains, "dp", axis=1, tiled=True),
    )
    qkv_w = back_weights[0][0][:, :split_at]
    out_w = back_weights[0][0][:, split_at:]
    ffn_w, gain_row = (back_weights[1][0], back_weights[2][0])
    grad_received = jnp.zeros_like(edge_data[0, 0])
    piece_list = []
    input_grad_list = []
    gain_total = jnp.zeros(gain_row.shape, jnp.float32)
    for tick_num in range(micro_count + 1):
        saved_state = pick_section(
            leading, saved_list[max(tick_num - 1, 0)], saved_list[min(tick_num + 1, micro_count)]
        )
        cosine_table, sine_values, allowed = pick_section(
            leading, table_list[max(tick_num - 1, 0)], table_list[min(tick_num, micro_count - 1)]
        )
        cotangent = edge_data[1, min(tick_num, micro_count - 1)]
        incoming = jnp.where(leading, grad_received, cotangent).astype(jnp.float32)
        is_valid = jnp.where(leading, tick_num >= 1, tick_num < micro_count)
        incoming = jnp.where(is_valid, incoming, 0.0)
        input_grad, pieces, gain_grad = layer_backward(
            incoming, saved_state, qkv_w, out_w, ffn_w, gain_row, cosine_table, sine_values, allowed
        )
        input_grad_list.append(input_grad)
        gain_total = gain_total + gain_grad
        piece_list.append(pieces)
        if tick_num < micro_count:
            grad_received = passed_along(input_grad.astype(jnp.bfloat16), "section", -1)
    owner_rows, owner_width, attn_share, ffn_share = owner_rows_maker(piece_list, owners)
    total_shard = lax.psum_scatter(
        owner_rows(jnp.int32(0), owner_width * lax.axis_size("dp")),
        "dp",
        scatter_dimension=0,
        tiled=True,
    )
    attention_shard, ffn_shard = unpack_shard(total_shard, attn_share, ffn_share)
    gain_shard = lax.psum_scatter(gain_total[None], "dp", scatter_dimension=1, tiled=True)
    edge_out = jnp.stack(
        [
            jnp.where(leading, input_grad_list[mb_num + 1], output_list[mb_num + 1])
            for mb_num in range(micro_count)
        ]
    ).astype(jnp.bfloat16)
    return (edge_out[None], attention_shard, ffn_shard, gain_shard)


def solution(mesh):
    in_specs = (
        P("section", None, "dp", None),
        P(None, "dp"),
        P("section", None, "dp"),
        P("section", None, None, "dp"),
        P("section", "dp"),
    )
    out_specs = (
        P("section", None, "dp", None),
        P("section", None, "dp"),
        P("section", None, None, "dp"),
        P("section", "dp"),
    )
    return jax.shard_map(local, mesh=mesh, in_specs=in_specs, out_specs=out_specs, check_vma=False)
```

profile of v0, /device:TPU:0, one launch (start us, length us, event | category | flops | bytes accessed | tf_op | source)
XLA Modules:
  0.0 897.1 jit_solution(8501034763040781893)
XLA Ops:
  8.7 1.3 fusion.218
  11.6 35.6 %all-reduce.14 = bf16[1920]{0:T(1024)(128)(2,1)S(1)} all-reduce(bf16[1920]{0:T(1024)(128)(2,1)S(1)} %dynamic-update-slice), channel_id=1, replica_groups=mesh['section'=2,'dp'=16] {'dp'}, use_global_device_ids=true, to_apply=%add.14 | all-reduce | flops 1920 | bytes 7680
  50.9 17.9 %all-gather.5.cloned.1.call-done = bf16[1,960,2560]{1,2,0:T(8,128)(2,1)} async-done(((bf16[1,960,160]{1,2,0:T(8,128)(2,1)}), bf16[1,960,2560]{1,2,0:T(8,128)(2,1)}) %all-gather.5.cloned.1.call-update) | async-done | bytes 4915216 | tf_op jit(solution)/shard_map/all_gather | solution.py:285
  68.8 3.1 fusion.55
  74.4 2.1 multiply_reduce_fusion.23
  76.6 113.0 %all-gather.3.cloned.1.call-done = bf16[1,3,960,2560]{2,3,1,0:T(8,128)(2,1)} async-done(((bf16[1,3,960,160]{2,3,1,0:T(8,128)(2,1)}), bf16[1,3,960,2560]{2,3,1,0:T(8,128)(2,1)}) %all-gather.3.cloned.1.call-update) | async-done | bytes 14745616 | tf_op jit(solution)/shard_map/all_gather | solution.py:310
  189.6 4.2 fusion.41
  193.8 5.3 multiply_convert_fusion.5
  199.1 3.6 fusion.92
  202.7 3.8 collective-permute-start
  210.0 3.1 fusion.53
  215.9 2.3 multiply_reduce_fusion.21
  219.0 4.3 fusion.40
  223.4 5.4 broadcast_select_fusion.2
  228.8 4.6 fusion.112
  234.6 1.7 multiply_reduce_fusion.7
  237.1 2.3 convolution_convert_fusion.5
  243.0 3.9 fusion.90
  247.0 4.4 collective-permute-start.2
  251.4 2.5 collective-permute-done.2
  253.9 4.1 multiply_reduce_fusion.8
  263.1 2.9 multiply_reduce_fusion.16
  268.5 1.7 fusion.136
  270.3 1.3 collective-permute-start.1
  273.7 4.3 fusion.38
  278.1 4.6 broadcast_select_fusion.1
  286.1 4.3 fusion.91
  291.0 1.7 broadcast_select_fusion.19
  292.7 4.5 fusion.115
  298.4 1.7 multiply_reduce_fusion.5
  300.8 2.3 convolution_convert_fusion.4
  309.7 3.4 multiply_reduce_fusion.6
  314.2 1.5 collective-permute-start.3
  317.3 4.3 collective-permute-done.3
  321.7 4.7 fusion.118
  326.5 3.8 fusion.30
  330.3 4.2 multiply_reduce_fusion.3
  335.4 2.3 convolution_convert_fusion.3
  339.8 2.4 pad_maximum_fusion
  345.0 5.3 fusion.60
  350.4 2.8 multiply_reduce_fusion.4
  354.6 133.8 %while.10 = (s32[]{:T(128)}, f32[16,640,960]{2,1,0:T(8,128)}, s32[16]{0:T(128)S(1)}, bf16[192,2560]{0,1:T(8,128)(2,1)}, bf16[192,960]{1,0:T(8,128)(2,1)S(1)}, /*...) while((s32[]{:T(128)}, f32[16,640,960]{2,1,0:T(8,128)}, ...), condition=%wide.region_30.31_spmd, body=%wide.region_29.30_spmd.sunk | while | flops 296908800 | bytes 11109091 | solution.py:258
  361.1 1.8 fusion.297
  369.4 1.8 fusion.297
  373.6 1.3 convolution_add_fusion.5
  377.8 1.9 fusion.297
  386.2 1.8 fusion.297
  394.5 1.9 fusion.297
  403.0 1.8 fusion.297
  407.1 1.3 convolution_add_fusion.5
  411.3 1.8 fusion.297
  419.6 1.9 fusion.297
  428.0 1.8 fusion.297
  436.4 1.9 fusion.297
  444.8 1.9 fusion.297
  453.3 1.8 fusion.297
  461.6 1.8 fusion.297
  469.9 1.9 fusion.297
  478.3 1.8 fusion.297
  486.6 1.8 fusion.297
  489.3 30.0 %all-reduce.15 = f32[1,1920]{1,0:T(1,128)S(1)} all-reduce(f32[1,1920]{1,0:T(1,128)S(1)} %fusion.191), channel_id=3, replica_groups=mesh['section'=2,'dp'=16] {'dp'}, use_global_device_ids=true, to_apply=%region_38.39.clone | all-reduce | flops 1920 | bytes 15360
  520.6 365.6 %reduce-scatter.3.cloned.1.call-done = f32[640,960]{1,0:T(8,128)} async-done(((f32[10240,960]{1,0:T(8,128)}), f32[640,960]{1,0:T(8,128)}) %reduce-scatter.3.cloned.1.call-update) | async-done | bytes 2457616 | tf_op jit(solution)/shard_map/reduce_scatter | solution.py:340
  886.2 2.7 slice_bitcast_fusion.37
  888.9 1.4 maximum_bitcast_fusion.1
  (501 shorter events, 143.9 us)
Async XLA Ops:
  7.2 61.7 %all-gather.5.cloned.1.call-start = ((), (), s32[]{:S(2)}) async-start(), calls=%async_computation.2 | async-start | bytes 5570560 | tf_op jit(solution)/shard_map/all_gather | solution.py:285
  7.9 181.7 %all-gather.3.cloned.1.call-start = ((), (), s32[]{:S(2)}) async-start(), calls=%async_computation.1 | async-start | bytes 16711680 | tf_op jit(solution)/shard_map/all_gather | solution.py:310
  8.6 877.5 %reduce-scatter.3.cloned.1.call-start = ((), (), s32[]{:S(2)}) async-start(), calls=%async_computation.3 | async-start | bytes 44564480 | tf_op jit(solution)/shard_map/reduce_scatter | solution.py:340
  49.2 23.0 %copy-start.73 = (f32[64]{0:T(128)}, f32[64]{0:T(128)S(1)}, u32[]{:S(2)}) copy-start(f32[64]{0:T(128)S(1)} %add_rsqrt_fusion.5) | copy-start | bytes 772
  49.3 160.7 %copy-start.58 = (f32[1,960]{1,0:T(1,128)}, f32[1,960]{1,0:T(1,128)S(1)}, u32[]{:S(2)}) copy-start(f32[1,960]{1,0:T(1,128)S(1)} %get-tuple-element.217) | copy-start | bytes 11524
  49.3 223.6 %copy-start.55 = (f32[1,960]{1,0:T(1,128)}, f32[1,960]{1,0:T(1,128)S(1)}, u32[]{:S(2)}) copy-start(f32[1,960]{1,0:T(1,128)S(1)} %get-tuple-element.216) | copy-start | bytes 11524
  50.9 209.6 %copy-start.15 = (f32[64,32]{1,0:T(8,128)}, f32[64,32]{1,0:T(8,128)S(1)}, u32[]{:S(2)}) copy-start(f32[64,32]{1,0:T(8,128)S(1)} %get-tuple-element.224) | copy-start | bytes 24580
  50.9 209.6 %copy-start.18 = (f32[64,32]{1,0:T(8,128)}, f32[64,32]{1,0:T(8,128)S(1)}, u32[]{:S(2)}) copy-start(f32[64,32]{1,0:T(8,128)S(1)} %get-tuple-element.225) | copy-start | bytes 24580
  76.6 141.7 %copy-start.83 = (f32[64]{0:T(128)}, f32[64]{0:T(128)S(1)}, u32[]{:S(2)}) copy-start(f32[64]{0:T(128)S(1)} %add_rsqrt_fusion.4) | copy-start | bytes 772
  193.8 8.9 copy-start.96
  199.1 14.0 %copy-start.101 = (bf16[64,2560]{1,0:T(8,128)(2,1)}, bf16[64,2560]{1,0:T(8,128)(2,1)S(1)}, u32[]{:S(2)}) copy-start(bf16[64,2560]{1,0:T(8,128)(2,1)S(1)} %get-tuple-element.238) | copy-start | bytes 983044
  202.7 6.5 collective-permute-start
  208.1 31.7 %copy-start.21 = (bf16[64,5,64]{2,0,1:T(8,128)(2,1)}, bf16[64,5,64]{2,0,1:T(8,128)(2,1)S(1)}, u32[]{:S(2)}) copy-start(bf16[64,5,64]{2,0,1:T(8,128)(2,1)S(1)} %copy.141) | copy-start | bytes 122884
  215.9 17.6 %slice-start.2 = ((s8[15728640]{0:T(1024)(128)(4,1)}), s8[4194304]{0:T(1024)(128)(4,1)S(1)}, s32[]{:S(2)}) async-start(s8[15728640]{0:T(1024)(128)(4,1)} %bitcast.493), calls=%async_computation.6 | async-start | bytes 8388608
  219.0 9.8 %copy-start.31 = (bf16[64,960]{1,0:T(8,128)(2,1)}, bf16[64,960]{1,0:T(8,128)(2,1)S(1)}, u32[]{:S(2)}) copy-start(bf16[64,960]{1,0:T(8,128)(2,1)S(1)} %get-tuple-element.137) | copy-start | bytes 368644
  219.0 14.5 %slice-start.3 = ((s8[15728640]{0:T(1024)(128)(4,1)}), s8[4194304]{0:T(1024)(128)(4,1)S(1)}, s32[]{:S(2)}) async-start(s8[15728640]{0:T(1024)(128)(4,1)} %bitcast.493), calls=%async_computation.7 | async-start | bytes 8388608
  223.4 10.1 %copy-start.99 = (f32[64,2560]{1,0:T(8,128)}, f32[64,2560]{1,0:T(8,128)S(1)}, u32[]{:S(2)}) copy-start(f32[64,2560]{1,0:T(8,128)S(1)} %fusion.40) | copy-start | bytes 1966084
  223.4 10.1 %slice-start.4 = ((s8[15728640]{0:T(1024)(128)(4,1)}), s8[4194304]{0:T(1024)(128)(4,1)S(1)}, s32[]{:S(2)}) async-start(s8[15728640]{0:T(1024)(128)(4,1)} %bitcast.493), calls=%async_computation.8 | async-start | bytes 8388608
  241.2 12.7 %copy-start.40 = (bf16[5,64,64]{2,1,0:T(8,128)(2,1)}, bf16[5,64,64]{2,1,0:T(8,128)(2,1)S(1)}, u32[]{:S(2)}) copy-start(bf16[5,64,64]{2,1,0:T(8,128)(2,1)S(1)} %fusion.99) | copy-start | bytes 122884
  242.2 9.1 %copy-start.91 = (f32[64]{0:T(128)S(1)}, f32[64]{0:T(128)}, u32[]{:S(2)}) copy-start(f32[64]{0:T(128)} %get-tuple-element.106) | copy-start | bytes 772
  242.2 11.6 %copy-start.59 = (f32[1,960]{1,0:T(1,128)S(1)}, f32[1,960]{1,0:T(1,128)}, u32[]{:S(2)}) copy-start(f32[1,960]{1,0:T(1,128)} %copy-done.58) | copy-start | bytes 11524
  242.6 15.3 %copy-start.13 = (bf16[64,5,3,64]{0,3,2,1:T(8,128)(2,1)}, bf16[64,5,3,64]{0,3,2,1:T(8,128)(2,1)S(1)}, u32[]{:S(2)}) copy-start(bf16[64,5,3,64]{0,3,2,1:T(8,128)(2,1)S(1)} %copy.148) | copy-start | bytes 368644
  243.0 15.0 %copy-start.42 = (bf16[64,5,64]{0,2,1:T(8,128)(2,1)}, bf16[64,5,64]{0,2,1:T(8,128)(2,1)S(1)}, u32[]{:S(2)}) copy-start(bf16[64,5,64]{0,2,1:T(8,128)(2,1)S(1)} %copy.152) | copy-start | bytes 122884
  243.0 15.0 %slice-start = ((s8[5242880]{0:T(1024)(128)(4,1)}), s8[4194304]{0:T(1024)(128)(4,1)S(1)}, s32[]{:S(2)}) async-start(s8[5242880]{0:T(1024)(128)(4,1)} %bitcast.421), calls=%async_computation.4 | async-start | bytes 8388608
  243.0 15.0 %slice-start.1 = ((s8[5242880]{0:T(1024)(128)(4,1)}), s8[1048576]{0:T(1024)(128)(4,1)S(1)}, s32[]{:S(2)}) async-start(s8[5242880]{0:T(1024)(128)(4,1)} %bitcast.421), calls=%async_computation.5 | async-start | bytes 2097152
  247.0 6.9 collective-permute-start.2
  260.4 8.1 copy-start.9
  260.5 44.0 %copy-start.1 = (bf16[64,5,64]{2,0,1:T(8,128)(2,1)}, bf16[64,5,64]{2,0,1:T(8,128)(2,1)S(1)}, u32[]{:S(2)}) copy-start(bf16[64,5,64]{2,0,1:T(8,128)(2,1)S(1)} %pad_maximum_fusion.13) | copy-start | bytes 122884
  260.5 11.8 %copy-start.94 = (f32[64]{0:T(128)S(1)}, f32[64]{0:T(128)}, u32[]{:S(2)}) copy-start(f32[64]{0:T(128)} %get-tuple-element.103) | copy-start | bytes 772
  260.6 12.3 %copy-start.84 = (f32[64]{0:T(128)S(1)}, f32[64]{0:T(128)}, u32[]{:S(2)}) copy-start(f32[64]{0:T(128)} %copy-done.83) | copy-start | bytes 772
  266.0 16.6 %copy-start.7 = (f32[64,960]{1,0:T(8,128)}, f32[64,960]{1,0:T(8,128)S(1)}, u32[]{:S(2)}) copy-start(f32[64,960]{1,0:T(8,128)S(1)} %get-tuple-element.250) | copy-start | bytes 737284
  266.0 24.4 %copy-start.87 = (f32[64]{0:T(128)}, f32[64]{0:T(128)S(1)}, u32[]{:S(2)}) copy-start(f32[64]{0:T(128)S(1)} %get-tuple-element.197) | copy-start | bytes 772
  270.3 20.7 %collective-permute-start.1 = (bf16[64,960]{1,0:T(8,128)(2,1)}, bf16[64,960]{1,0:T(8,128)(2,1)}, u32[]{:S(2)}, u32[]{:S(2)}) collective-permute-start(bf16[64,960]{1,0:T(8,128)(2,1)} %fusion.136), channel_id=1, source_target_pairs={{16,0},{17,1},{18,2},{19,3},{20,4},{21,5},{22,6},{23,7},{24,8},{25... | collective-permute-start | bytes 368648 | tf_op jit(solution)/shard_map/ppermute | solution.py:18
  271.6 28.5 %copy-start.79 = (f32[64]{0:T(128)}, f32[64]{0:T(128)S(1)}, u32[]{:S(2)}) copy-start(f32[64]{0:T(128)S(1)} %fusion.194) | copy-start | bytes 772
  273.7 23.6 %slice-start.6 = ((s8[15728640]{0:T(1024)(128)(4,1)}), s8[4194304]{0:T(1024)(128)(4,1)S(1)}, s32[]{:S(2)}) async-start(s8[15728640]{0:T(1024)(128)(4,1)} %bitcast.495), calls=%async_computation.10 | async-start | bytes 8388608
  278.0 14.7 %copy-start.100 = (f32[64,2560]{1,0:T(8,128)}, f32[64,2560]{1,0:T(8,128)S(1)}, u32[]{:S(2)}) copy-start(f32[64,2560]{1,0:T(8,128)S(1)} %fusion.38) | copy-start | bytes 1966084
  278.1 19.2 %slice-start.7 = ((s8[15728640]{0:T(1024)(128)(4,1)}), s8[4194304]{0:T(1024)(128)(4,1)S(1)}, s32[]{:S(2)}) async-start(s8[15728640]{0:T(1024)(128)(4,1)} %bitcast.495), calls=%async_computation.11 | async-start | bytes 8388608
  282.7 10.0 %copy-start.104 = (f32[64,2560]{1,0:T(8,128)}, f32[64,2560]{1,0:T(8,128)S(1)}, u32[]{:S(2)}) copy-start(f32[64,2560]{1,0:T(8,128)S(1)} %get-tuple-element.251) | copy-start | bytes 1966084
  283.1 7.9 copy-start.60
  283.1 7.9 copy-start.71
  283.1 7.9 copy-start.74
  284.2 8.5 copy-start.98
  284.2 8.5 copy-start.106
  284.2 13.1 %slice-start.8 = ((s8[15728640]{0:T(1024)(128)(4,1)}), s8[4194304]{0:T(1024)(128)(4,1)S(1)}, s32[]{:S(2)}) async-start(s8[15728640]{0:T(1024)(128)(4,1)} %bitcast.495), calls=%async_computation.12 | async-start | bytes 8388608
  305.3 8.9 copy-start.41
  305.3 7.8 copy-start.4
  305.4 7.8 copy-start.12
  306.5 9.2 %copy-start.92 = (f32[64]{0:T(128)S(1)}, f32[64]{0:T(128)}, u32[]{:S(2)}) copy-start(f32[64]{0:T(128)} %get-tuple-element.104) | copy-start | bytes 772
  309.7 12.0 %copy-start.43 = (bf16[64,5,64]{0,2,1:T(8,128)(2,1)}, bf16[64,5,64]{0,2,1:T(8,128)(2,1)S(1)}, u32[]{:S(2)}) copy-start(bf16[64,5,64]{0,2,1:T(8,128)(2,1)S(1)} %copy.173) | copy-start | bytes 122884
  314.2 7.4 collective-permute-start.3
  326.4 8.1 copy-start.50
  326.4 8.1 copy-start.52
  326.5 8.1 copy-start.88
  330.3 8.0 copy-start.2
  339.8 10.6 %copy-start.5 = (bf16[64,960]{1,0:T(8,128)(2,1)S(1)}, bf16[64,960]{1,0:T(8,128)(2,1)}, u32[]{:S(2)}) copy-start(bf16[64,960]{1,0:T(8,128)(2,1)} %copy-done.3) | copy-start | bytes 368644
  339.8 10.6 %copy-start.62 = (f32[1,960]{1,0:T(1,128)S(1)}, f32[1,960]{1,0:T(1,128)}, u32[]{:S(2)}) copy-start(f32[1,960]{1,0:T(1,128)} %copy-done.58) | copy-start | bytes 11524
  339.8 10.6 %copy-start.89 = (f32[64]{0:T(128)S(1)}, f32[64]{0:T(128)}, u32[]{:S(2)}) copy-start(f32[64]{0:T(128)} %fusion.197) | copy-start | bytes 772
  342.6 10.7 %copy-start.93 = (f32[64]{0:T(128)S(1)}, f32[64]{0:T(128)}, u32[]{:S(2)}) copy-start(f32[64]{0:T(128)} %get-tuple-element.104) | copy-start | bytes 772
  342.6 10.7 %copy-start.72 = (f32[64]{0:T(128)S(1)}, f32[64]{0:T(128)}, u32[]{:S(2)}) copy-start(f32[64]{0:T(128)} %copy-done.70) | copy-start | bytes 772
  342.6 10.7 %copy-start.78 = (f32[64]{0:T(128)S(1)}, f32[64]{0:T(128)}, u32[]{:S(2)}) copy-start(f32[64]{0:T(128)} %copy-done.76) | copy-start | bytes 772
  343.5 9.8 %copy-start.10 = (f32[64,960]{1,0:T(8,128)S(1)}, f32[64,960]{1,0:T(8,128)}, u32[]{:S(2)}) copy-start(f32[64,960]{1,0:T(8,128)} %get-tuple-element.145) | copy-start | bytes 737284
  343.5 10.0 %copy-start.28 = (bf16[64,960]{1,0:T(8,128)(2,1)S(1)}, bf16[64,960]{1,0:T(8,128)(2,1)}, u32[]{:S(2)}) copy-start(bf16[64,960]{1,0:T(8,128)(2,1)} %bitcast_convert_fusion) | copy-start | bytes 368644
  343.5 10.0 %copy-start.30 = (bf16[64,960]{1,0:T(8,128)(2,1)S(1)}, bf16[64,960]{1,0:T(8,128)(2,1)}, u32[]{:S(2)}) copy-start(bf16[64,960]{1,0:T(8,128)(2,1)} %copy-done.29) | copy-start | bytes 368644
  488.4 31.4 %copy-start.39 = (bf16[1,1,64,960]{3,2,1,0:T(8,128)(2,1)S(1)}, bf16[1,1,64,960]{3,2,1,0:T(8,128)(2,1)}, u32[]{:S(2)}) copy-start(bf16[1,1,64,960]{3,2,1,0:T(8,128)(2,1)} %get-tuple-element.140) | copy-start | bytes 368644
  (60 other events, 261.1 us)
Sparse Core Ops, SparseCore 0:
  10.3 58.5 all-gather.4
  71.1 118.4 all-gather.2
  488.6 397.5 reduce-scatter.2
where the time goes:
time: 905 us; the launch traced here: 897 us
  waiting for transfers between devices  506 us (56%)
  matrix products  192 us (21%)
  other arithmetic  67 us (7%)
  blocking collectives  65.5 us (7%)
  local copies, waits for them, and re-layouts  27.3 us (3%)
  between operations  17.5 us (2%)
  loops' own time  11.2 us (1%)
  starting transfers between devices  11.1 us (1%)
    reduce_scatter x1, waiting for transfers between devices, local(): lax.psum_scatter(owner_rows(jnp.int32(0), owner_width * lax.axis_size('dp...  366 us
    all_gather x1, waiting for transfers between devices, local(): lax.all_gather(ffn_weight, 'dp', axis=3, tiled=True)  113 us
    dot_general x80, matrix products, left_trans(): lax.dot_general(left_op, right_op, contract_first, preferred_element_type...  83.9 us
    unnamed x2, blocking collectives  65.5 us
    dot_general x15, matrix products, matmul(): return jnp.dot(left_op, right_op, preferred_element_type=jnp.float32)  56.2 us
    dot_general x15, matrix products, right_trans(): lax.dot_general(left_op, right_op, contract_last, preferred_element_type=...  43 us
    dynamic_update_slice x16, other arithmetic, owner_rows(): stacked = lax.map(one_owner, owner_list)  29.5 us
  transfers between devices with their start and end apart: 7, of which 6 were waited for; matrix products, arithmetic and copies ran while one was open for 4% of the time, Pallas kernels for 0%

commit v1 on v0

--- a/solution.py
+++ b/solution.py
@@ -10,6 +10,27 @@
 theta_base = 100000.0
 contract_last = (((1,), (1,)), ((), ()))
 contract_first = (((0,), (0,)), ((), ()))
+
+
+def collect(value, axis, dim):
+    peers, position, rows = (lax.axis_size(axis), lax.axis_index(axis), value.shape[dim])
+    forward = [(i, (i + 1) % peers) for i in range(peers)]
+    backward = [(i, (i - 1) % peers) for i in range(peers)]
+    whole = jnp.zeros((*value.shape[:dim], peers * rows, *value.shape[dim + 1 :]), value.dtype)
+    whole = lax.dynamic_update_slice_in_dim(whole, value, position * rows, axis=dim)
+    from_left = from_right = value
+    halfway = peers // 2
+    for step in range(1, halfway + 1):
+        from_left = lax.ppermute(from_left, axis, forward)
+        whole = lax.dynamic_update_slice_in_dim(
+            whole, from_left, (position - step) % peers * rows, axis=dim
+        )
+        if step < peers - halfway:
+            from_right = lax.ppermute(from_right, axis, backward)
+            whole = lax.dynamic_update_slice_in_dim(
+                whole, from_right, (position + step) % peers * rows, axis=dim
+            )
+    return whole
 
 
 def passed_along(array, axis, by):
@@ -307,7 +328,7 @@
             received = passed_along(output.astype(jnp.bfloat16), "section", 1)
     back_weights = (
         lax.all_gather(attn_weight, "dp", axis=2, tiled=True),
-        lax.all_gather(ffn_weight, "dp", axis=3, tiled=True),
+        collect(ffn_weight, "dp", 3),
         lax.all_gather(gains, "dp", axis=1, tiled=True),
     )
     qkv_w = back_weights[0][0][:, :split_at]

time: 905 us -> 1030 us (1.14)
  starting transfers between devices: 11.1 us -> 113 us
  local copies, waits for them, and re-layouts: 27.3 us -> 62.8 us
  waiting for transfers between devices: 506 us -> 478 us
    all_gather x1, waiting for transfers between devices: 113 us -> 0.02 us  [local(): lax.all_gather(ffn_weight, 'dp', axis=3, tiled=True)]
    ppermute x0 -> x15, waiting for transfers between devices: none -> 101 us  [the longest x8 56 us: collect(): from_left = lax.ppermute(from_left, axis, forward)]
    ppermute x0 -> x15, starting transfers between devices: none -> 101 us  [the longest x8 81.9 us: collect(): from_left = lax.ppermute(from_left, axis, forward)]
    dynamic_update_slice x0 -> x16, local copies, waits for them, and re-layouts: none -> 22.5 us  [the longest x8 11.9 us: collect(): lax.dynamic_update_slice_in_dim(whole, from_left, (position - step) % pee...]
    all_gather x1, waiting for transfers between devices: 17.9 us -> 0.01 us  [local(): lax.all_gather(attn_weight, 'dp', axis=2, tiled=True)]
  transfers between devices with their start and end apart: 7 -> 22, of which waited for: 6 -> 11; matrix products, arithmetic and copies ran while one was open for 4% -> 8% of each run, Pallas kernels for 0% -> 0%
where the time goes in v1:
time: 1030 us; the launch traced here: 1020 us
  waiting for transfers between devices  478 us (46%)
  matrix products  199 us (19%)
  starting transfers between devices  113 us (11%)
  other arithmetic  70.1 us (7%)
  blocking collectives  64.9 us (6%)
  local copies, waits for them, and re-layouts  62.8 us (6%)
  between operations  17.7 us (2%)
  loops' own time  11.2 us (1%)
    reduce_scatter x1, waiting for transfers between devices, local(): lax.psum_scatter(owner_rows(jnp.int32(0), owner_width * lax.axis_size('dp...  368 us
    dot_general x80, matrix products, left_trans(): lax.dot_general(left_op, right_op, contract_first, preferred_element_type...  83.9 us
    ppermute x8, starting transfers between devices, collect(): from_left = lax.ppermute(from_left, axis, forward)  81.9 us
    unnamed x2, blocking collectives  64.9 us
    ppermute x8, waiting for transfers between devices, collect(): from_left = lax.ppermute(from_left, axis, forward)  56 us
    dot_general x15, matrix products, matmul(): return jnp.dot(left_op, right_op, preferred_element_type=jnp.float32)  53.5 us
    dot_general x15, matrix products, right_trans(): lax.dot_general(left_op, right_op, contract_last, preferred_element_type=...  53 us
    ppermute x7, waiting for transfers between devices, collect(): from_right = lax.ppermute(from_right, axis, backward)  45.1 us
  transfers between devices with their start and end apart: 22, of which 11 were waited for; matrix products, arithmetic and copies ran while one was open for 8% of the time, Pallas kernels for 0%

profile of v1, /device:TPU:0, one launch (start us, length us, event | category | flops | bytes accessed | tf_op | source)
XLA Modules:
  0.0 1016.4 jit_solution(14970435185553513047)
XLA Ops:
  9.2 5.0 collective-permute-start.1
  14.3 12.2 %collective-permute-done = bf16[1,3,960,160]{2,3,1,0:T(8,128)(2,1)} collective-permute-done((bf16[1,3,960,160]{2,3,1,0:T(8,128)(2,1)}, bf16[1,3,960,160]{2,3,1,0:T(8,128)(2,1)}, u32[]{:S(2)}, u32[]{:S(2)}) %collective-permute-start) | collective-permute-done | bytes 921632 | tf_op jit(solution)/shard_map/ppermute | solution.py:24
  26.5 10.7 %collective-permute-start.2 = (bf16[1,3,960,160]{2,3,1,0:T(8,128)(2,1)}, bf16[1,3,960,160]{2,3,1,0:T(8,128)(2,1)S(1)}, u32[]{:S(2)}, u32[]{:S(2)}) collective-permute-start(bf16[1,3,960,160]{2,3,1,0:T(8,128)(2,1)} %collective-permute-done), channel_id=1, source_target_pairs={{0,1},{1,2},{2,3},{3,4},{4,5},{5,6},{6,7},{7,8},{8,9},{9,10},{10,1... | collective-permute-start | bytes 2764808 | tf_op jit(solution)/shard_map/ppermute | solution.py:24
  39.1 9.8 collective-permute-done.2
  48.9 25.8 %collective-permute-start.4 = (bf16[1,3,960,160]{2,3,1,0:T(8,128)(2,1)S(1)}, bf16[1,3,960,160]{2,3,1,0:T(8,128)(2,1)}, u32[]{:S(2)}, u32[]{:S(2)}) collective-permute-start(bf16[1,3,960,160]{2,3,1,0:T(8,128)(2,1)S(1)} %collective-permute-done.2), channel_id=1, source_target_pairs={{0,1},{1,2},{2,3},{3,4},{4,5},{5,6},{6,7},{7,8},{8,9},{9,10},{10,1... | collective-permute-start | bytes 2764808 | tf_op jit(solution)/shard_map/ppermute | solution.py:24
  77.6 33.4 %all-reduce.14 = bf16[1920]{0:T(1024)(128)(2,1)S(1)} all-reduce(bf16[1920]{0:T(1024)(128)(2,1)S(1)} %dynamic-update-slice), channel_id=1, replica_groups=mesh['section'=2,'dp'=16] {'dp'}, use_global_device_ids=true, to_apply=%add.14 | all-reduce | flops 1920 | bytes 7680
  114.1 29.9 %collective-permute-done.5 = bf16[1,3,960,160]{2,3,1,0:T(8,128)(2,1)} collective-permute-done((bf16[1,3,960,160]{2,3,1,0:T(8,128)(2,1)S(1)}, bf16[1,3,960,160]{2,3,1,0:T(8,128)(2,1)}, u32[]{:S(2)}, u32[]{:S(2)}) %collective-permute-start.5) | collective-permute-done | bytes 921632 | tf_op jit(solution)/shard_map/ppermute | solution.py:29
  144.0 4.7 collective-permute-start.7
  149.7 7.4 squeeze.84
  158.2 2.3 bitcast_dynamic-update-slice_fusion.14
  160.5 2.9 collective-permute-done.7
  163.5 4.7 collective-permute-start.9
  171.3 24.3 %collective-permute-done.8 = bf16[1,3,960,160]{2,3,1,0:T(8,128)(2,1)S(1)} collective-permute-done((bf16[1,3,960,160]{2,3,1,0:T(8,128)(2,1)}, bf16[1,3,960,160]{2,3,1,0:T(8,128)(2,1)S(1)}, u32[]{:S(2)}, u32[]{:S(2)}) %collective-permute-start.8) | collective-permute-done | bytes 921632 | tf_op jit(solution)/shard_map/ppermute | solution.py:24
  195.6 2.4 collective-permute-start.10
  198.0 2.2 bitcast_dynamic-update-slice_fusion.10
  201.3 4.5 collective-permute-start.11
  205.8 2.2 bitcast_dynamic-update-slice_fusion.9
  208.0 2.2 bitcast_dynamic-update-slice_fusion.8
  210.2 2.2 bitcast_dynamic-update-slice_fusion.7
  212.5 9.7 collective-permute-done.10
  222.2 27.4 %collective-permute-start.12 = (bf16[1,3,960,160]{2,3,1,0:T(8,128)(2,1)S(1)}, bf16[1,3,960,160]{2,3,1,0:T(8,128)(2,1)S(1)}, u32[]{:S(2)}, u32[]{:S(2)}) collective-permute-start(bf16[1,3,960,160]{2,3,1,0:T(8,128)(2,1)S(1)} %collective-permute-done.10), channel_id=1, source_target_pairs={{0,1},{1,2},{2,3},{3,4},{4,5},{5,6},{6,7},{7,8},{8,9},{9,10},{10,1... | collective-permute-start | bytes 2764808 | tf_op jit(solution)/shard_map/ppermute | solution.py:24
  253.6 14.5 %collective-permute-start.14 = (bf16[1,3,960,160]{2,3,1,0:T(8,128)(2,1)S(1)}, bf16[1,3,960,160]{2,3,1,0:T(8,128)(2,1)S(1)}, u32[]{:S(2)}, u32[]{:S(2)}) collective-permute-start(bf16[1,3,960,160]{2,3,1,0:T(8,128)(2,1)S(1)} %collective-permute-done.12), channel_id=1, source_target_pairs={{0,1},{1,2},{2,3},{3,4},{4,5},{5,6},{6,7},{7,8},{8,9},{9,10},{10,1... | collective-permute-start | bytes 2764808 | tf_op jit(solution)/shard_map/ppermute | solution.py:24
  269.1 11.1 %collective-permute-done.13 = bf16[1,3,960,160]{2,3,1,0:T(8,128)(2,1)S(1)} collective-permute-done((bf16[1,3,960,160]{2,3,1,0:T(8,128)(2,1)S(1)}, bf16[1,3,960,160]{2,3,1,0:T(8,128)(2,1)S(1)}, u32[]{:S(2)}, u32[]{:S(2)}) %collective-permute-start.13) | collective-permute-done | bytes 921632 | tf_op jit(solution)/shard_map/ppermute | solution.py:29
  281.3 3.1 fusion.55
  291.3 2.1 multiply_reduce_fusion.23
  293.5 4.2 fusion.23
  297.7 5.3 multiply_convert_fusion.5
  303.0 3.6 fusion.92
  306.7 4.3 collective-permute-start.15
  313.8 3.1 fusion.53
  319.4 2.3 multiply_reduce_fusion.21
  322.5 4.3 fusion.22
  326.9 5.4 broadcast_select_fusion.2
  332.3 4.6 fusion.112
  341.4 2.3 convolution_convert_fusion.5
  347.5 14.9 %fusion.90 = bf16[64,960]{1,0:T(8,128)(2,1)S(1)} fusion(f32[64,960]{1,0:T(8,128)S(1)} %get-tuple-element.242, bf16[64,2560]{1,0:T(8,128)(2,1)} %get-tuple-element.133, bf16[1,3,960,2560]{2,3,1,0:T(8,128)(2,1)} %all-gather.5.cloned.1.call-done), kind=kOutput, calls=%fused_computation.119 | convolution fusion | flops 314695680 | bytes 5939200 | tf_op jit(solution)/shard_map/dot_general | solution.py:47
  362.4 4.9 collective-permute-start.17
  367.4 2.5 collective-permute-done.17
  369.9 4.1 multiply_reduce_fusion.8
  380.6 2.9 multiply_reduce_fusion.16
  391.3 4.3 fusion.21
  395.8 4.6 broadcast_select_fusion.1
  403.7 4.3 fusion.91
  410.4 1.9 fusion.115
  415.7 2.3 convolution_convert_fusion.4
  424.7 2.9 multiply_reduce_fusion.6
  431.2 4.9 collective-permute-done.18
  436.2 4.7 fusion.118
  441.0 3.8 fusion.30
  444.8 3.7 multiply_reduce_fusion.3
  450.1 2.3 convolution_convert_fusion.3
  454.4 2.4 pad_maximum_fusion
  459.6 5.3 fusion.60
  464.9 2.8 multiply_reduce_fusion.4
  469.7 133.9 %while.10 = (s32[]{:T(128)}, f32[16,640,960]{2,1,0:T(8,128)}, s32[16]{0:T(128)S(1)}, bf16[192,2560]{0,1:T(8,128)(2,1)}, bf16[192,960]{1,0:T(8,128)(2,1)S(1)}, /*...) while((s32[]{:T(128)}, f32[16,640,960]{2,1,0:T(8,128)}, ...), condition=%wide.region_30.31_spmd, body=%wide.region_29.30_spmd.sunk | while | flops 296908800 | bytes 11109091 | solution.py:279
  484.6 1.9 fusion.297
  493.0 1.9 fusion.297
  509.7 1.8 fusion.297
  551.5 1.9 fusion.297
  559.9 1.9 fusion.297
  585.0 1.9 fusion.297
  604.4 31.4 %all-reduce.15 = f32[1,1920]{1,0:T(1,128)S(1)} all-reduce(f32[1,1920]{1,0:T(1,128)S(1)} %fusion.191), channel_id=3, replica_groups=mesh['section'=2,'dp'=16] {'dp'}, use_global_device_ids=true, to_apply=%region_38.39.clone | all-reduce | flops 1920 | bytes 15360
  637.2 368.2 %reduce-scatter.3.cloned.1.call-done = f32[640,960]{1,0:T(8,128)} async-done(((f32[10240,960]{1,0:T(8,128)}), f32[640,960]{1,0:T(8,128)}) %reduce-scatter.3.cloned.1.call-update) | async-done | bytes 2457616 | tf_op jit(solution)/shard_map/reduce_scatter | solution.py:361
  1005.4 2.7 slice_bitcast_fusion.40
  (562 shorter events, 198.0 us)
Async XLA Ops:
  7.2 274.1 %all-gather.3.cloned.1.call-start = ((), (), s32[]{:S(2)}) async-start(), calls=%async_computation.1 | async-start | bytes 5570560 | tf_op jit(solution)/shard_map/all_gather | solution.py:306
  7.9 285.6 %all-gather.5.cloned.1.call-start = ((), (), s32[]{:S(2)}) async-start(), calls=%async_computation.2 | async-start | bytes 16711680 | tf_op jit(solution)/shard_map/all_gather | solution.py:307
  8.6 996.7 %reduce-scatter.3.cloned.1.call-start = ((), (), s32[]{:S(2)}) async-start(), calls=%async_computation.3 | async-start | bytes 44564480 | tf_op jit(solution)/shard_map/reduce_scatter | solution.py:361
  8.7 17.8 %collective-permute-start = (bf16[1,3,960,160]{2,3,1,0:T(8,128)(2,1)}, bf16[1,3,960,160]{2,3,1,0:T(8,128)(2,1)}, u32[]{:S(2)}, u32[]{:S(2)}) collective-permute-start(bf16[1,3,960,160]{2,3,1,0:T(8,128)(2,1)} %param.10), channel_id=1, source_target_pairs={{0,1},{1,2},{2,3},{3,4},{4,5},{5,6},{6,7},{7,8},{8,9},{9,10},{10,1... | collective-permute-start | bytes 2764808 | tf_op jit(solution)/shard_map/ppermute | solution.py:24
  9.2 28.0 %collective-permute-start.1 = (bf16[1,3,960,160]{2,3,1,0:T(8,128)(2,1)}, bf16[1,3,960,160]{2,3,1,0:T(8,128)(2,1)S(1)}, u32[]{:S(2)}, u32[]{:S(2)}) collective-permute-start(bf16[1,3,960,160]{2,3,1,0:T(8,128)(2,1)} %param.10), channel_id=1, source_target_pairs={{0,15},{1,0},{2,1},{3,2},{4,3},{5,4},{6,5},{7,6},{8,7},{9,8},{10,9... | collective-permute-start | bytes 2764808 | tf_op jit(solution)/shard_map/ppermute | solution.py:29
  26.5 22.4 %collective-permute-start.2 = (bf16[1,3,960,160]{2,3,1,0:T(8,128)(2,1)}, bf16[1,3,960,160]{2,3,1,0:T(8,128)(2,1)S(1)}, u32[]{:S(2)}, u32[]{:S(2)}) collective-permute-start(bf16[1,3,960,160]{2,3,1,0:T(8,128)(2,1)} %collective-permute-done), channel_id=1, source_target_pairs={{0,1},{1,2},{2,3},{3,4},{4,5},{5,6},{6,7},{7,8},{8,9},{9,10},{10,1... | collective-permute-start | bytes 2764808 | tf_op jit(solution)/shard_map/ppermute | solution.py:24
  37.3 73.8 %collective-permute-start.3 = (bf16[1,3,960,160]{2,3,1,0:T(8,128)(2,1)S(1)}, bf16[1,3,960,160]{2,3,1,0:T(8,128)(2,1)S(1)}, u32[]{:S(2)}, u32[]{:S(2)}) collective-permute-start(bf16[1,3,960,160]{2,3,1,0:T(8,128)(2,1)S(1)} %collective-permute-done.1), channel_id=1, source_target_pairs={{0,15},{1,0},{2,1},{3,2},{4,3},{5,4},{6,5},{7,6},{8,7},{9,8},{10,9... | collective-permute-start | bytes 2764808 | tf_op jit(solution)/shard_map/ppermute | solution.py:29
  38.3 243.0 %copy-start.75 = (f32[64]{0:T(128)}, f32[64]{0:T(128)S(1)}, u32[]{:S(2)}) copy-start(f32[64]{0:T(128)S(1)} %add_rsqrt_fusion.5) | copy-start | bytes 772
  48.9 64.7 %collective-permute-start.4 = (bf16[1,3,960,160]{2,3,1,0:T(8,128)(2,1)S(1)}, bf16[1,3,960,160]{2,3,1,0:T(8,128)(2,1)}, u32[]{:S(2)}, u32[]{:S(2)}) collective-permute-start(bf16[1,3,960,160]{2,3,1,0:T(8,128)(2,1)S(1)} %collective-permute-done.2), channel_id=1, source_target_pairs={{0,1},{1,2},{2,3},{3,4},{4,5},{5,6},{6,7},{7,8},{8,9},{9,10},{10,1... | collective-permute-start | bytes 2764808 | tf_op jit(solution)/shard_map/ppermute | solution.py:24
  111.1 37.7 %copy-start.13 = (bf16[1,3,960,160]{2,3,1,0:T(8,128)(2,1)}, bf16[1,3,960,160]{2,3,1,0:T(8,128)(2,1)S(1)}, u32[]{:S(2)}) copy-start(bf16[1,3,960,160]{2,3,1,0:T(8,128)(2,1)S(1)} %collective-permute-done.3) | copy-start | bytes 2764804
  111.1 32.9 %collective-permute-start.5 = (bf16[1,3,960,160]{2,3,1,0:T(8,128)(2,1)S(1)}, bf16[1,3,960,160]{2,3,1,0:T(8,128)(2,1)}, u32[]{:S(2)}, u32[]{:S(2)}) collective-permute-start(bf16[1,3,960,160]{2,3,1,0:T(8,128)(2,1)S(1)} %collective-permute-done.3), channel_id=1, source_target_pairs={{0,15},{1,0},{2,1},{3,2},{4,3},{5,4},{6,5},{7,6},{8,7},{9,8},{10,9... | collective-permute-start | bytes 2764808 | tf_op jit(solution)/shard_map/ppermute | solution.py:29
  111.2 228.6 %copy-start.60 = (f32[1,960]{1,0:T(1,128)}, f32[1,960]{1,0:T(1,128)S(1)}, u32[]{:S(2)}) copy-start(f32[1,960]{1,0:T(1,128)S(1)} %get-tuple-element.216) | copy-start | bytes 11524
  111.2 262.7 %copy-start.64 = (f32[1,960]{1,0:T(1,128)}, f32[1,960]{1,0:T(1,128)S(1)}, u32[]{:S(2)}) copy-start(f32[1,960]{1,0:T(1,128)S(1)} %get-tuple-element.217) | copy-start | bytes 11524
  113.6 44.6 %collective-permute-start.6 = (bf16[1,3,960,160]{2,3,1,0:T(8,128)(2,1)}, bf16[1,3,960,160]{2,3,1,0:T(8,128)(2,1)}, u32[]{:S(2)}, u32[]{:S(2)}) collective-permute-start(bf16[1,3,960,160]{2,3,1,0:T(8,128)(2,1)} %collective-permute-done.4), channel_id=1, source_target_pairs={{0,1},{1,2},{2,3},{3,4},{4,5},{5,6},{6,7},{7,8},{8,9},{9,10},{10,1... | collective-permute-start | bytes 2764808 | tf_op jit(solution)/shard_map/ppermute | solution.py:24
  144.0 19.5 %collective-permute-start.7 = (bf16[1,3,960,160]{2,3,1,0:T(8,128)(2,1)}, bf16[1,3,960,160]{2,3,1,0:T(8,128)(2,1)}, u32[]{:S(2)}, u32[]{:S(2)}) collective-permute-start(bf16[1,3,960,160]{2,3,1,0:T(8,128)(2,1)} %collective-permute-done.5), channel_id=1, source_target_pairs={{0,15},{1,0},{2,1},{3,2},{4,3},{5,4},{6,5},{7,6},{8,7},{9,8},{10,9... | collective-permute-start | bytes 2764808 | tf_op jit(solution)/shard_map/ppermute | solution.py:29
  149.7 227.2 %copy-start.17 = (f32[64,32]{1,0:T(8,128)}, f32[64,32]{1,0:T(8,128)S(1)}, u32[]{:S(2)}) copy-start(f32[64,32]{1,0:T(8,128)S(1)} %get-tuple-element.224) | copy-start | bytes 24580
  149.7 227.2 %copy-start.19 = (f32[64,32]{1,0:T(8,128)}, f32[64,32]{1,0:T(8,128)S(1)}, u32[]{:S(2)}) copy-start(f32[64,32]{1,0:T(8,128)S(1)} %get-tuple-element.225) | copy-start | bytes 24580
  157.2 13.1 %copy-start.14 = (bf16[1,3,960,160]{2,3,1,0:T(8,128)(2,1)S(1)}, bf16[1,3,960,160]{2,3,1,0:T(8,128)(2,1)}, u32[]{:S(2)}) copy-start(bf16[1,3,960,160]{2,3,1,0:T(8,128)(2,1)} %copy-done.13) | copy-start | bytes 2764804
  158.2 37.4 %collective-permute-start.8 = (bf16[1,3,960,160]{2,3,1,0:T(8,128)(2,1)}, bf16[1,3,960,160]{2,3,1,0:T(8,128)(2,1)S(1)}, u32[]{:S(2)}, u32[]{:S(2)}) collective-permute-start(bf16[1,3,960,160]{2,3,1,0:T(8,128)(2,1)} %collective-permute-done.6), channel_id=1, source_target_pairs={{0,1},{1,2},{2,3},{3,4},{4,5},{5,6},{6,7},{7,8},{8,9},{9,10},{10,1... | collective-permute-start | bytes 2764808 | tf_op jit(solution)/shard_map/ppermute | solution.py:24
  163.5 37.9 %collective-permute-start.9 = (bf16[1,3,960,160]{2,3,1,0:T(8,128)(2,1)}, bf16[1,3,960,160]{2,3,1,0:T(8,128)(2,1)S(1)}, u32[]{:S(2)}, u32[]{:S(2)}) collective-permute-start(bf16[1,3,960,160]{2,3,1,0:T(8,128)(2,1)} %collective-permute-done.7), channel_id=1, source_target_pairs={{0,15},{1,0},{2,1},{3,2},{4,3},{5,4},{6,5},{7,6},{8,7},{9,8},{10,9... | collective-permute-start | bytes 2764808 | tf_op jit(solution)/shard_map/ppermute | solution.py:29
  195.6 26.6 %collective-permute-start.10 = (bf16[1,3,960,160]{2,3,1,0:T(8,128)(2,1)S(1)}, bf16[1,3,960,160]{2,3,1,0:T(8,128)(2,1)S(1)}, u32[]{:S(2)}, u32[]{:S(2)}) collective-permute-start(bf16[1,3,960,160]{2,3,1,0:T(8,128)(2,1)S(1)} %collective-permute-done.8), channel_id=1, source_target_pairs={{0,1},{1,2},{2,3},{3,4},{4,5},{5,6},{6,7},{7,8},{8,9},{9,10},{10,1... | collective-permute-start | bytes 2764808 | tf_op jit(solution)/shard_map/ppermute | solution.py:24
  201.3 49.2 %collective-permute-start.11 = (bf16[1,3,960,160]{2,3,1,0:T(8,128)(2,1)S(1)}, bf16[1,3,960,160]{2,3,1,0:T(8,128)(2,1)S(1)}, u32[]{:S(2)}, u32[]{:S(2)}) collective-permute-start(bf16[1,3,960,160]{2,3,1,0:T(8,128)(2,1)S(1)} %collective-permute-done.9), channel_id=1, source_target_pairs={{0,15},{1,0},{2,1},{3,2},{4,3},{5,4},{6,5},{7,6},{8,7},{9,8},{10,9... | collective-permute-start | bytes 2764808 | tf_op jit(solution)/shard_map/ppermute | solution.py:29
  222.2 31.4 %collective-permute-start.12 = (bf16[1,3,960,160]{2,3,1,0:T(8,128)(2,1)S(1)}, bf16[1,3,960,160]{2,3,1,0:T(8,128)(2,1)S(1)}, u32[]{:S(2)}, u32[]{:S(2)}) collective-permute-start(bf16[1,3,960,160]{2,3,1,0:T(8,128)(2,1)S(1)} %collective-permute-done.10), channel_id=1, source_target_pairs={{0,1},{1,2},{2,3},{3,4},{4,5},{5,6},{6,7},{7,8},{8,9},{9,10},{10,1... | collective-permute-start | bytes 2764808 | tf_op jit(solution)/shard_map/ppermute | solution.py:24
  250.5 30.8 %copy-start = (bf16[1,2,64,960]{3,2,1,0:T(8,128)(2,1)S(1)}, bf16[1,2,64,960]{3,2,1,0:T(8,128)(2,1)}, u32[]{:S(2)}) copy-start(bf16[1,2,64,960]{3,2,1,0:T(8,128)(2,1)} %param.7) | copy-start | bytes 737284
  250.5 29.7 %collective-permute-start.13 = (bf16[1,3,960,160]{2,3,1,0:T(8,128)(2,1)S(1)}, bf16[1,3,960,160]{2,3,1,0:T(8,128)(2,1)S(1)}, u32[]{:S(2)}, u32[]{:S(2)}) collective-permute-start(bf16[1,3,960,160]{2,3,1,0:T(8,128)(2,1)S(1)} %collective-permute-done.11), channel_id=1, source_target_pairs={{0,15},{1,0},{2,1},{3,2},{4,3},{5,4},{6,5},{7,6},{8,7},{9,8},{10,9... | collective-permute-start | bytes 2764808 | tf_op jit(solution)/shard_map/ppermute | solution.py:29
  253.6 57.3 %collective-permute-start.14 = (bf16[1,3,960,160]{2,3,1,0:T(8,128)(2,1)S(1)}, bf16[1,3,960,160]{2,3,1,0:T(8,128)(2,1)S(1)}, u32[]{:S(2)}, u32[]{:S(2)}) collective-permute-start(bf16[1,3,960,160]{2,3,1,0:T(8,128)(2,1)S(1)} %collective-permute-done.12), channel_id=1, source_target_pairs={{0,1},{1,2},{2,3},{3,4},{4,5},{5,6},{6,7},{7,8},{8,9},{9,10},{10,1... | collective-permute-start | bytes 2764808 | tf_op jit(solution)/shard_map/ppermute | solution.py:24
  306.7 6.3 collective-permute-start.15
  312.9 31.4 %copy-start.23 = (bf16[64,5,64]{2,0,1:T(8,128)(2,1)}, bf16[64,5,64]{2,0,1:T(8,128)(2,1)S(1)}, u32[]{:S(2)}) copy-start(bf16[64,5,64]{2,0,1:T(8,128)(2,1)S(1)} %copy.141) | copy-start | bytes 122884
  319.4 17.6 %slice-start = ((s8[15728640]{0:T(1024)(128)(4,1)}), s8[4194304]{0:T(1024)(128)(4,1)S(1)}, s32[]{:S(2)}) async-start(s8[15728640]{0:T(1024)(128)(4,1)} %bitcast.448), calls=%async_computation.4 | async-start | bytes 8388608
  322.5 14.5 %slice-start.1 = ((s8[15728640]{0:T(1024)(128)(4,1)}), s8[4194304]{0:T(1024)(128)(4,1)S(1)}, s32[]{:S(2)}) async-start(s8[15728640]{0:T(1024)(128)(4,1)} %bitcast.448), calls=%async_computation.5 | async-start | bytes 8388608
  326.8 10.1 copy-start.106
  326.9 10.1 slice-start.2
  345.7 24.2 %copy-start.43 = (bf16[5,64,64]{2,1,0:T(8,128)(2,1)}, bf16[5,64,64]{2,1,0:T(8,128)(2,1)S(1)}, u32[]{:S(2)}) copy-start(bf16[5,64,64]{2,1,0:T(8,128)(2,1)S(1)} %fusion.99) | copy-start | bytes 122884
  346.8 20.6 %copy-start.98 = (f32[64]{0:T(128)S(1)}, f32[64]{0:T(128)}, u32[]{:S(2)}) copy-start(f32[64]{0:T(128)} %get-tuple-element.106) | copy-start | bytes 772
  347.1 26.8 %copy-start.15 = (bf16[64,5,3,64]{0,3,2,1:T(8,128)(2,1)}, bf16[64,5,3,64]{0,3,2,1:T(8,128)(2,1)S(1)}, u32[]{:S(2)}) copy-start(bf16[64,5,3,64]{0,3,2,1:T(8,128)(2,1)S(1)} %copy.148) | copy-start | bytes 368644
  347.5 26.4 %copy-start.45 = (bf16[64,5,64]{0,2,1:T(8,128)(2,1)}, bf16[64,5,64]{0,2,1:T(8,128)(2,1)S(1)}, u32[]{:S(2)}) copy-start(bf16[64,5,64]{0,2,1:T(8,128)(2,1)S(1)} %copy.152) | copy-start | bytes 122884
  347.5 26.5 %slice-start.8 = ((s8[5242880]{0:T(1024)(128)(4,1)}), s8[4194304]{0:T(1024)(128)(4,1)S(1)}, s32[]{:S(2)}) async-start(s8[5242880]{0:T(1024)(128)(4,1)} %bitcast.463), calls=%async_computation.12 | async-start | bytes 8388608
  347.5 26.5 %slice-start.9 = ((s8[5242880]{0:T(1024)(128)(4,1)}), s8[1048576]{0:T(1024)(128)(4,1)S(1)}, s32[]{:S(2)}) async-start(s8[5242880]{0:T(1024)(128)(4,1)} %bitcast.463), calls=%async_computation.13 | async-start | bytes 2097152
  362.4 7.4 collective-permute-start.17
  377.1 42.4 %copy-start.2 = (bf16[64,5,64]{2,0,1:T(8,128)(2,1)}, bf16[64,5,64]{2,0,1:T(8,128)(2,1)S(1)}, u32[]{:S(2)}) copy-start(bf16[64,5,64]{2,0,1:T(8,128)(2,1)S(1)} %pad_maximum_fusion.13) | copy-start | bytes 122884
  377.1 12.8 %copy-start.101 = (f32[64]{0:T(128)S(1)}, f32[64]{0:T(128)}, u32[]{:S(2)}) copy-start(f32[64]{0:T(128)} %get-tuple-element.103) | copy-start | bytes 772
  377.1 13.4 %copy-start.61 = (f32[1,960]{1,0:T(1,128)S(1)}, f32[1,960]{1,0:T(1,128)}, u32[]{:S(2)}) copy-start(f32[1,960]{1,0:T(1,128)} %copy-done.60) | copy-start | bytes 11524
  377.2 13.4 %copy-start.90 = (f32[64]{0:T(128)S(1)}, f32[64]{0:T(128)}, u32[]{:S(2)}) copy-start(f32[64]{0:T(128)} %copy-done.88) | copy-start | bytes 772
  383.5 16.8 %copy-start.8 = (f32[64,960]{1,0:T(8,128)}, f32[64,960]{1,0:T(8,128)S(1)}, u32[]{:S(2)}) copy-start(f32[64,960]{1,0:T(8,128)S(1)} %get-tuple-element.250) | copy-start | bytes 737284
  383.5 24.5 %copy-start.93 = (f32[64]{0:T(128)}, f32[64]{0:T(128)S(1)}, u32[]{:S(2)}) copy-start(f32[64]{0:T(128)S(1)} %get-tuple-element.197) | copy-start | bytes 772
  387.9 20.7 %collective-permute-start.16 = (bf16[64,960]{1,0:T(8,128)(2,1)}, bf16[64,960]{1,0:T(8,128)(2,1)}, u32[]{:S(2)}, u32[]{:S(2)}) collective-permute-start(bf16[64,960]{1,0:T(8,128)(2,1)} %fusion.136), channel_id=1, source_target_pairs={{16,0},{17,1},{18,2},{19,3},{20,4},{21,5},{22,6},{23,7},{24,8},{25... | collective-permute-start | bytes 368648 | tf_op jit(solution)/shard_map/ppermute | solution.py:39
  389.2 25.9 %copy-start.84 = (f32[64]{0:T(128)}, f32[64]{0:T(128)S(1)}, u32[]{:S(2)}) copy-start(f32[64]{0:T(128)S(1)} %fusion.194) | copy-start | bytes 772
  391.3 19.0 %slice-start.4 = ((s8[15728640]{0:T(1024)(128)(4,1)}), s8[4194304]{0:T(1024)(128)(4,1)S(1)}, s32[]{:S(2)}) async-start(s8[15728640]{0:T(1024)(128)(4,1)} %bitcast.450), calls=%async_computation.8 | async-start | bytes 8388608
  395.7 14.6 %copy-start.107 = (f32[64,2560]{1,0:T(8,128)}, f32[64,2560]{1,0:T(8,128)S(1)}, u32[]{:S(2)}) copy-start(f32[64,2560]{1,0:T(8,128)S(1)} %fusion.21) | copy-start | bytes 1966084
  395.7 14.6 %slice-start.5 = ((s8[15728640]{0:T(1024)(128)(4,1)}), s8[4194304]{0:T(1024)(128)(4,1)S(1)}, s32[]{:S(2)}) async-start(s8[15728640]{0:T(1024)(128)(4,1)} %bitcast.450), calls=%async_computation.9 | async-start | bytes 8388608
  395.7 14.6 %slice-start.6 = ((s8[15728640]{0:T(1024)(128)(4,1)}), s8[4194304]{0:T(1024)(128)(4,1)S(1)}, s32[]{:S(2)}) async-start(s8[15728640]{0:T(1024)(128)(4,1)} %bitcast.450), calls=%async_computation.10 | async-start | bytes 8388608
  400.3 10.0 copy-start.111
  423.5 17.4 %copy-start.16 = (bf16[64,5,3,64]{0,3,2,1:T(8,128)(2,1)}, bf16[64,5,3,64]{0,3,2,1:T(8,128)(2,1)S(1)}, u32[]{:S(2)}) copy-start(bf16[64,5,3,64]{0,3,2,1:T(8,128)(2,1)S(1)} %copy.169) | copy-start | bytes 368644
  424.6 16.2 %copy-start.46 = (bf16[64,5,64]{0,2,1:T(8,128)(2,1)}, bf16[64,5,64]{0,2,1:T(8,128)(2,1)S(1)}, u32[]{:S(2)}) copy-start(bf16[64,5,64]{0,2,1:T(8,128)(2,1)S(1)} %copy.173) | copy-start | bytes 122884
  428.6 7.5 collective-permute-start.18
  454.4 10.5 %copy-start.6 = (bf16[64,960]{1,0:T(8,128)(2,1)S(1)}, bf16[64,960]{1,0:T(8,128)(2,1)}, u32[]{:S(2)}) copy-start(bf16[64,960]{1,0:T(8,128)(2,1)} %copy-done.4) | copy-start | bytes 368644
  454.4 10.5 %copy-start.67 = (f32[1,960]{1,0:T(1,128)S(1)}, f32[1,960]{1,0:T(1,128)}, u32[]{:S(2)}) copy-start(f32[1,960]{1,0:T(1,128)} %copy-done.64) | copy-start | bytes 11524
  457.1 10.6 %copy-start.100 = (f32[64]{0:T(128)S(1)}, f32[64]{0:T(128)}, u32[]{:S(2)}) copy-start(f32[64]{0:T(128)} %get-tuple-element.104) | copy-start | bytes 772
  457.1 10.6 %copy-start.80 = (f32[64]{0:T(128)S(1)}, f32[64]{0:T(128)}, u32[]{:S(2)}) copy-start(f32[64]{0:T(128)} %copy-done.78) | copy-start | bytes 772
  457.1 10.6 %copy-start.83 = (f32[64]{0:T(128)S(1)}, f32[64]{0:T(128)}, u32[]{:S(2)}) copy-start(f32[64]{0:T(128)} %copy-done.81) | copy-start | bytes 772
  458.0 10.6 %copy-start.30 = (bf16[64,960]{1,0:T(8,128)(2,1)S(1)}, bf16[64,960]{1,0:T(8,128)(2,1)}, u32[]{:S(2)}) copy-start(bf16[64,960]{1,0:T(8,128)(2,1)} %bitcast_convert_fusion) | copy-start | bytes 368644
  458.0 10.6 %copy-start.32 = (bf16[64,960]{1,0:T(8,128)(2,1)S(1)}, bf16[64,960]{1,0:T(8,128)(2,1)}, u32[]{:S(2)}) copy-start(bf16[64,960]{1,0:T(8,128)(2,1)} %copy-done.31) | copy-start | bytes 368644
  603.6 32.9 %copy-start.35 = (bf16[1,1,64,960]{3,2,1,0:T(8,128)(2,1)S(1)}, bf16[1,1,64,960]{3,2,1,0:T(8,128)(2,1)}, u32[]{:S(2)}) copy-start(bf16[1,1,64,960]{3,2,1,0:T(8,128)(2,1)} %get-tuple-element.194) | copy-start | bytes 368644
  603.6 32.9 %copy-start.42 = (bf16[1,1,64,960]{3,2,1,0:T(8,128)(2,1)S(1)}, bf16[1,1,64,960]{3,2,1,0:T(8,128)(2,1)}, u32[]{:S(2)}) copy-start(bf16[1,1,64,960]{3,2,1,0:T(8,128)(2,1)} %get-tuple-element.140) | copy-start | bytes 368644
  (82 other events, 460.0 us)
Sparse Core Ops, SparseCore 0:
  10.3 86.2 all-gather.2
  98.8 186.1 all-gather.4
  603.7 401.5 reduce-scatter.2
